TPU v7x, 256 devices: a whole 4x4x8 slice. The times are simulated.
256 devices in a mesh: grp: 8 (over y, core), dom: 32 (over x, z).
Axes of the slice: x: 4, y: 4, z: 8, core: 2. Of those that a mesh axis runs over, the one named last changes fastest.
Arguments:
- fine_nodes: bfloat16 [8, 24576, 128], P('grp', 'dom'), may hold values from -6 to 6
- fine_edges: bfloat16 [8, 294912, 128], P('grp', 'dom'), may hold values from -6 to 6
- fine_senders: int32 [8, 294912], P('grp', 'dom'), may hold values from 0 to 1535
- fine_receivers: int32 [8, 294912], P('grp', 'dom'), may hold values from 0 to 767, as said below
- edge_count: int32 [8, 32], P('grp', 'dom'), may hold values from 4608 to 9216, as said below
- ghost_send: int32 [8, 1024, 24], P('grp', 'dom'), may hold values from 0 to 767
- fine_parent: int32 [8, 24576], P('grp', 'dom'), may hold values from 0 to 16383, as said below
- coarse_nodes: bfloat16 [16384, 128], P('dom'), may hold values from -6 to 6
- coarse_edges: bfloat16 [131072, 128], P('dom'), may hold values from -6 to 6
- coarse_senders: int32 [131072], P('dom'), may hold values from 0 to 16383
- coarse_receivers: int32 [131072], P('dom'), may hold values from 0 to 511, as said below
- edge_in: bfloat16 [2, 384, 128], replicated, may hold values from -0.3125 to 0.3125
- node_in: bfloat16 [3, 256, 128], replicated, may hold values from -0.375 to 0.375
- mlp_out: bfloat16 [5, 128, 128], replicated, may hold values from -0.5 to 0.5
Outputs:
- fine_out: bfloat16 [8, 24576, 128], P('grp', 'dom')
- coarse_out: bfloat16 [16384, 128], P('dom')
Inputs may be any that keep to these rules, and one draw needn't show every extreme that they name: `edge_count`: each device's live edge slot count; slots from that count on are padding; 9216 on at least one device. `fine_receivers`: nondecreasing along each device's 9216 slots; padding slots hold 767. `fine_senders`: below 768: a local node; 768 + s * 24 + k: ghost slot k received from dom index s of the same slab. `ghost_send`: local node indices; row p of a device's block lists the nodes sent to dom index p. `fine_parent`: global coarse index; owner o holds coarse nodes o * 512 to (o + 1) * 512 - 1. Most parents of a fine node of dom index d are owned by d itself; the others may be owned by any owner. `coarse_senders`: global coarse index of the sender. `coarse_receivers`: nondecreasing within each owner's 4096 edges.
All inputs are finite; a program needn't handle non-finite values.
Results may differ from a plain program's by a relative error of at most 0.015.
Values may be sent and summed in bfloat16 or wider, within the bound.
A program may use at most 64 MiB of HBM per device.

v0:
```python
import math
import jax
import jax.numpy as jnp
from jax import lax
from jax.sharding import Mesh
from jax.sharding import PartitionSpec as P

DOM = ("dom_0", "dom_1")


def in_blocks(array, dim, peers):
    shape = array.shape
    blocks = array.reshape(*shape[:dim], peers, shape[dim] // peers, *shape[dim + 1 :])
    return jnp.moveaxis(blocks, dim, 0)


def summed_on_arrival(array, axis, dim):
    peers = lax.axis_size(axis)
    blocks = lax.all_to_all(in_blocks(array, dim, peers), axis, 0, 0, tiled=True)
    return jnp.sum(blocks.astype(jnp.float32), axis=0)


def side_by_side(arrays, axis, dim, along):
    widths = [math.prod(a.shape[along:]) for a in arrays]
    both = jnp.concatenate(
        [a.reshape(*a.shape[:along], w) for a, w in zip(arrays, widths)], axis=along
    )
    out = summed_on_arrival(both, axis, dim)
    blocks = jnp.split(out, [sum(widths[:k]) for k in range(1, len(widths))], axis=along)
    return tuple((b.reshape(*out.shape[:along], *a.shape[along:]) for a, b in zip(arrays, blocks)))


def joined_along(blocks, dim):
    shape = list(blocks.shape[1:])
    shape[dim] *= blocks.shape[0]
    return jnp.moveaxis(blocks, 0, dim).reshape(shape)


def copy_for_each(array, axis):
    peers = lax.axis_size(axis)
    return lax.all_to_all(
        jnp.broadcast_to(array[None], (peers, *array.shape)), axis, 0, 0, tiled=True
    )


def gather_directly(array, axis, dim):
    return joined_along(copy_for_each(array, axis), dim)


def sent_together(arrays, axis, dim, along):
    widths = [math.prod(a.shape[along:]) for a in arrays]
    both = jnp.concatenate(
        [a.reshape(*a.shape[:along], w) for a, w in zip(arrays, widths)], axis=along
    )
    out = gather_directly(both, axis, dim)
    blocks = jnp.split(out, [sum(widths[:k]) for k in range(1, len(widths))], axis=along)
    return tuple((b.reshape(*out.shape[:along], *a.shape[along:]) for a, b in zip(arrays, blocks)))


def gather_in_order(array, axes, order):
    blocks = array[None]
    for k in order:
        blocks = lax.all_gather(blocks, axes[k], axis=0, tiled=True)
    current = [lax.axis_size(axes[k]) for k in reversed(order)]
    blocks = blocks.reshape(*current, *array.shape)
    turned = sorted(range(len(order)), key=lambda place: order[len(order) - 1 - place])
    return blocks.transpose(*turned, *range(len(order), blocks.ndim)).reshape(-1, *array.shape)


def whole_of(array, axes, order, dim):
    return joined_along(gather_in_order(array, axes, order), dim)


def layer_norm(values):
    centre = values - jnp.mean(values, -1, keepdims=True)
    spread = jnp.mean(centre * centre, -1, keepdims=True)
    return centre * lax.rsqrt(spread + 1e-05)


def perceptron(inputs, w_first, w_second):
    hidden = jax.nn.silu(jnp.dot(inputs, w_first, preferred_element_type=jnp.float32)).astype(
        jnp.bfloat16
    )
    return layer_norm(jnp.dot(hidden, w_second, preferred_element_type=jnp.float32))


def per_device(
    fine_nodes,
    fine_edges,
    fine_senders,
    fine_receivers,
    edge_count,
    ghost_send,
    fine_parent,
    coarse_nodes,
    coarse_edges,
    coarse_senders,
    coarse_receivers,
    edge_in,
    node_in,
    mlp_out,
):
    domains = lax.axis_size(DOM)
    groups = lax.axis_size("grp")
    local = fine_nodes[0]
    node_rows, width = local.shape
    owner_rows = coarse_nodes.shape[0]
    coarse_total = owner_rows * domains
    outgoing = local[ghost_send[0]]
    incoming = lax.all_to_all(outgoing, DOM, split_axis=0, concat_axis=0, tiled=True)
    table = jnp.concatenate([local, incoming.reshape(-1, width)], 0)
    edges = fine_edges[0]
    receivers = fine_receivers[0]
    inputs = jnp.concatenate([edges, local[receivers], table[fine_senders[0]]], -1)
    edge_new = edges.astype(jnp.float32) + perceptron(inputs, edge_in[0], mlp_out[0])
    live = (jnp.arange(edges.shape[0]) < edge_count[0, 0]).astype(jnp.float32)
    summed = jax.ops.segment_sum(
        edge_new * live[:, None], receivers, num_segments=node_rows
    ).astype(jnp.bfloat16)
    fine_mid = (
        local.astype(jnp.float32)
        + perceptron(jnp.concatenate([local, summed], -1), node_in[0], mlp_out[1])
    ).astype(jnp.bfloat16)
    parents = fine_parent[0]
    ones_rows = jnp.ones(parents.shape, jnp.float32)
    mid_wide = fine_mid.astype(jnp.float32)
    piece = owner_rows // groups
    owner = parents // owner_rows
    within = parents % owner_rows
    mapped = within // piece * (domains * piece) + owner * piece + within % piece
    pooled = jax.ops.segment_sum(mid_wide, mapped, num_segments=coarse_total).reshape(
        groups, domains, piece, width
    )
    children = jax.ops.segment_sum(ones_rows, mapped, num_segments=coarse_total).reshape(
        groups, domains, piece
    )
    pooled, children = (
        lax.psum_scatter(
            pooled.astype(jnp.bfloat16), "grp", scatter_dimension=0, tiled=True
        ).astype(jnp.float32),
        lax.psum_scatter(
            children.astype(jnp.bfloat16), "grp", scatter_dimension=0, tiled=True
        ).astype(jnp.float32),
    )
    pooled, children = side_by_side(
        (pooled.astype(jnp.bfloat16), children.astype(jnp.bfloat16)), DOM, 1, 3
    )
    pooled, children = sent_together((pooled, children), "grp", 0, 3)
    pooled = pooled.reshape(owner_rows, width)
    children = children.reshape(owner_rows)
    coarse_mid = ((coarse_nodes.astype(jnp.float32) + pooled) / (1.0 + children)[:, None]).astype(
        jnp.bfloat16
    )
    coarse_table = whole_of(coarse_mid, DOM, (0, 1), 0)
    cinputs = jnp.concatenate(
        [coarse_edges, coarse_mid[coarse_receivers], coarse_table[coarse_senders]], -1
    )
    cedge_new = coarse_edges.astype(jnp.float32) + perceptron(cinputs, edge_in[1], mlp_out[2])
    csummed = jax.ops.segment_sum(cedge_new, coarse_receivers, num_segments=owner_rows).astype(
        jnp.bfloat16
    )
    coarse_out = (
        coarse_mid.astype(jnp.float32)
        + perceptron(jnp.concatenate([coarse_mid, csummed], -1), node_in[1], mlp_out[3])
    ).astype(jnp.bfloat16)
    updated_table = whole_of(coarse_out, DOM, (0, 1), 0)
    above = updated_table[parents]
    fine_out = (
        mid_wide + perceptron(jnp.concatenate([fine_mid, above], -1), node_in[2], mlp_out[4])
    ).astype(jnp.bfloat16)
    return (fine_out[None], coarse_out)


def solution(mesh):
    torus = Mesh(mesh.devices.reshape(mesh.shape["grp"], 4, 8), ("grp", "dom_0", "dom_1"))
    in_specs = (
        P("grp", DOM, None),
        P("grp", DOM, None),
        P("grp", DOM),
        P("grp", DOM),
        P("grp", DOM),
        P("grp", DOM, None),
        P("grp", DOM),
        P(DOM, None),
        P(DOM, None),
        P(DOM),
        P(DOM),
        P(),
        P(),
        P(),
    )
    out_specs = (P("grp", DOM, None), P(DOM, None))
    return jax.shard_map(
        per_device, mesh=torus, in_specs=in_specs, out_specs=out_specs, check_vma=False
    )
```

profile of v0, /device:TPU:1, one launch (start us, length us, event | category | flops | bytes accessed | tf_op | source)
XLA Modules:
  0.0 494.9 jit_solution(16880242438352926247)
XLA Ops:
  8.1 3.2 gather_fusion.1
  11.4 11.9 %all-to-all-start = ((bf16[32,24,128]{2,1,0:T(8,128)(2,1)}), bf16[32,24,128]{2,1,0:T(8,128)(2,1)S(1)}, u32[]{:S(2)}, u32[]{:S(2)}) async-start(bf16[32,24,128]{2,1,0:T(8,128)(2,1)} %bitcast.8), calls=%async_computation | async-start | bytes 393216 | tf_op jit(solution)/shard_map/all_to_all | solution.py:110
  24.0 4.6 scatter_custom_fusion.2
  32.2 27.0 %gather_fusion = bf16[9216,128]{1,0:T(8,128)(2,1)S(1)} fusion(bf16[768,128]{1,0:T(8,128)(2,1)S(1)} %bitcast.111, s32[9216]{0:T(1024)S(1)} %broadcast_clamp_fusion.1), kind=kCustom, calls=%fused_computation | custom fusion | bytes 4755456 | tf_op jit(solution)/shard_map/gather | solution.py:114
  59.2 2.5 copy.87
  61.7 4.3 copy.81
  67.1 27.0 %gather_fusion.2 = bf16[9216,128]{1,0:T(8,128)(2,1)S(1)} fusion(bf16[1536,128]{1,0:T(8,128)(2,1)S(1)} %copy.86, s32[9216]{0:T(1024)S(1)} %broadcast_clamp_fusion), kind=kCustom, calls=%fused_computation.2 | custom fusion | bytes 4755456 | tf_op jit(solution)/shard_map/gather | solution.py:114
  94.1 2.5 copy.88
  96.6 6.8 %fusion.114 = (f32[9216]{0:T(1024)S(1)}, f32[9216,128]{0,1:T(8,128)}) fusion(bf16[5,128,128]{2,1,0:T(8,128)(2,1)} %param.27, bf16[9216,128]{0,1:T(8,128)(2,1)} %copy.88, bf16[9216,128]{0,1:T(8,128)(2,1)} %copy.87, bf16[9216,128]{0,1:T(8,128)(2,1)} %bitcast.114, bf16[2,384,128]{2,1,0:T(8,128)(2,1)S(1)} %copy-done.7), kind=kOutput, calls=%fused_computation.141 | convolution fusion | flops 1236261888 | bytes 11964416 | tf_op jit(solution)/shard_map/dot_general | solution.py:84
  103.4 3.0 multiply_reduce_fusion
  107.2 3.0 add_multiply_fusion
  110.2 6.1 %copy.89 = f32[9216,128]{1,0:T(8,128)} copy(f32[9216,128]{0,1:T(8,128)} %add_multiply_fusion) | data formatting | bytes 9437184 | tf_op jit(solution)/shard_map/mul | solution.py:118
  116.3 61.0 %scatter_custom_fusion = f32[768,128]{1,0:T(8,128)S(1)} fusion(s32[9216]{0:T(1024)} %bitcast.128, f32[9216,128]{1,0:T(8,128)} %copy.89, f32[]{:T(128)} %constant.85.clone.1), kind=kCustom, calls=%fused_computation.68 | custom fusion | flops 1179648 | bytes 393728 | tf_op jit(solution)/shard_map/scatter-add | solution.py:117
  179.0 9.7 %scatter_custom_fusion.1 = f32[16384,128]{1,0:T(8,128)} fusion(s32[768]{0:T(1024)S(1)} %get-tuple-element.11, f32[768,128]{1,0:T(8,128)S(1)} %copy.92, f32[]{:T(128)} %constant.85.clone.1), kind=kCustom, calls=%fused_computation.19 | custom fusion | flops 98304 | bytes 8388612 | tf_op jit(solution)/shard_map/scatter-add | solution.py:131
  188.8 5.1 %convert_element_type.86 = bf16[16384,128]{1,0:T(8,128)(2,1)} convert(f32[16384,128]{1,0:T(8,128)} %scatter_custom_fusion.1) | non-fusion elementwise | flops 2097152 | bytes 12582912 | tf_op jit(solution)/shard_map/convert_element_type | solution.py:139
  195.0 38.6 %reduce-scatter.3.cloned.1.call-done = bf16[1,32,64,128]{3,2,1,0:T(8,128)(2,1)} async-done(((bf16[8,32,64,128]{3,2,1,0:T(8,128)(2,1)}), bf16[1,32,64,128]{3,2,1,0:T(8,128)(2,1)}) %reduce-scatter.3.cloned.1.call-update) | async-done | bytes 524304 | tf_op jit(solution)/shard_map/reduce_scatter | solution.py:138
  234.9 30.8 %all_to_all.15 = bf16[32,1,1,64,129]{4,3,2,1,0:T(8,128)(2,1)S(1)} all-to-all(bf16[32,1,1,64,129]{4,3,2,1,0:T(8,128)(2,1)S(1)} %maximum_bitcast_fusion), channel_id=1, replica_groups=mesh['grp'=8,'dom_0'=4,'dom_1'=8] {'dom_0','dom_1'}, dimensions={0} | all-to-all | bytes 1056768 | tf_op jit(solution)/shard_map/all_to_all | solution.py:19
  266.7 12.0 %all-to-all-start.2 = ((f32[8,1,1,64,129]{4,3,2,1,0:T(8,128)}), f32[8,1,1,64,129]{4,3,2,1,0:T(8,128)S(1)}, u32[]{:S(2)}, u32[]{:S(2)}) async-start(f32[8,1,1,64,129]{4,3,2,1,0:T(8,128)} %broadcast_in_dim.28), calls=%async_computation.4 | async-start | bytes 1048576 | tf_op jit(solution)/shard_map/all_to_all | solution.py:41
  278.9 9.2 %all-to-all-done.2 = f32[8,1,1,64,129]{4,3,2,1,0:T(8,128)S(1)} async-done(((f32[8,1,1,64,129]{4,3,2,1,0:T(8,128)}), f32[8,1,1,64,129]{4,3,2,1,0:T(8,128)S(1)}, u32[]{:S(2)}, u32[]{:S(2)}) %all-to-all-start.2) | async-done | bytes 264224 | tf_op jit(solution)/shard_map/all_to_all | solution.py:41
  288.5 9.9 %all-gather = bf16[2048,128]{0,1:T(8,128)(2,1)S(1)} all-gather(bf16[512,128]{0,1:T(8,128)(2,1)S(1)} %divide_convert_fusion), channel_id=2, replica_groups=mesh['grp'=8,'dom_0'=4,'dom_1'=8] {'dom_0'}, dimensions={0}, use_global_device_ids=true | all-gather | bytes 655360 | tf_op jit(solution)/shard_map/all_gather | solution.py:63
  300.4 14.9 %gather_fusion.3 = bf16[4096,128]{1,0:T(8,128)(2,1)} fusion(bf16[512,128]{1,0:T(8,128)(2,1)S(1)} %copy.96, s32[4096]{0:T(1024)S(1)} %fusion.94), kind=kCustom, calls=%fused_computation.3 | custom fusion | bytes 2113536 | tf_op jit(solution)/shard_map/gather | solution.py:156
  315.3 37.2 %all-gather.5.cloned.1.call-done = bf16[32,512,128]{2,1,0:T(8,128)(2,1)} async-done(((bf16[4,512,128]{2,1,0:T(8,128)(2,1)}), bf16[32,512,128]{2,1,0:T(8,128)(2,1)}) %all-gather.5.cloned.1.call-update) | async-done | bytes 4194320 | tf_op jit(solution)/shard_map/all_gather | solution.py:63
  352.5 4.6 copy.98
  357.1 17.0 %gather_fusion.4 = bf16[4096,128]{1,0:T(8,128)(2,1)} fusion(bf16[16384,128]{1,0:T(8,128)(2,1)} %bitcast.112, s32[4096]{0:T(1024)S(1)} %fusion.95), kind=kCustom, calls=%fused_computation.4 | custom fusion | bytes 2113536 | tf_op jit(solution)/shard_map/gather | solution.py:156
  374.1 3.3 fusion.124
  377.7 1.7 multiply_add_fusion
  379.4 1.9 copy.99
  381.3 26.5 %scatter_custom_fusion.3 = f32[512,128]{1,0:T(8,128)S(1)} fusion(s32[4096]{0:T(1024)S(1)} %copy-done.6, f32[4096,128]{1,0:T(8,128)S(1)} %copy.99, f32[]{:T(128)} %constant.85.clone.1), kind=kCustom, calls=%fused_computation.71 | custom fusion | flops 524288 | bytes 262148 | tf_op jit(solution)/shard_map/scatter-add | solution.py:159
  409.3 11.7 %all-gather.1 = bf16[2048,128]{0,1:T(8,128)(2,1)S(1)} all-gather(bf16[512,128]{0,1:T(8,128)(2,1)S(1)} %add_convert_fusion.2), channel_id=3, replica_groups=mesh['grp'=8,'dom_0'=4,'dom_1'=8] {'dom_0'}, dimensions={0}, use_global_device_ids=true | all-gather | bytes 655360 | tf_op jit(solution)/shard_map/all_gather | solution.py:63
  422.7 54.3 %all-gather.7.cloned.1.call-done = bf16[32,512,128]{2,1,0:T(8,128)(2,1)} async-done(((bf16[4,512,128]{2,1,0:T(8,128)(2,1)}), bf16[32,512,128]{2,1,0:T(8,128)(2,1)}) %all-gather.7.cloned.1.call-update) | async-done | bytes 4194320 | tf_op jit(solution)/shard_map/all_gather | solution.py:63
  477.0 4.6 copy.102
  481.6 4.3 gather_fusion.5
  (88 shorter events, 19.8 us)
Async XLA Ops:
  7.2 25.0 %copy-start = (bf16[1,768,128]{2,1,0:T(8,128)(2,1)S(1)}, bf16[1,768,128]{2,1,0:T(8,128)(2,1)}, u32[]{:S(2)}) copy-start(bf16[1,768,128]{2,1,0:T(8,128)(2,1)} %param.14) | copy-start | bytes 589828
  11.4 55.3 %all-to-all-start = ((bf16[32,24,128]{2,1,0:T(8,128)(2,1)}), bf16[32,24,128]{2,1,0:T(8,128)(2,1)S(1)}, u32[]{:S(2)}, u32[]{:S(2)}) async-start(bf16[32,24,128]{2,1,0:T(8,128)(2,1)} %bitcast.8), calls=%async_computation | async-start | bytes 393216 | tf_op jit(solution)/shard_map/all_to_all | solution.py:110
  23.2 170.7 %reduce-scatter.5.cloned.1.call-start = ((), (), s32[]{:S(2)}) async-start(), calls=%async_computation.6 | async-start | bytes 73728 | tf_op jit(solution)/shard_map/reduce_scatter | solution.py:141
  29.4 204.2 %reduce-scatter.3.cloned.1.call-start = ((), (), s32[]{:S(2)}) async-start(), calls=%async_computation.5 | async-start | bytes 4718592 | tf_op jit(solution)/shard_map/reduce_scatter | solution.py:138
  94.1 2.5 copy-start.7
  96.6 9.8 %copy-start.2 = (bf16[1,9216,128]{1,2,0:T(8,128)(2,1)S(1)}, bf16[1,9216,128]{1,2,0:T(8,128)(2,1)}, u32[]{:S(2)}) copy-start(bf16[1,9216,128]{1,2,0:T(8,128)(2,1)} %copy.81) | copy-start | bytes 7077892
  103.4 3.8 copy-start.1
  195.0 83.8 %copy-start.4 = (bf16[512,128]{1,0:T(8,128)(2,1)S(1)}, bf16[512,128]{1,0:T(8,128)(2,1)}, u32[]{:S(2)}) copy-start(bf16[512,128]{1,0:T(8,128)(2,1)} %param.21) | copy-start | bytes 393220
  265.8 33.9 %copy-start.3 = (bf16[4096,128]{1,0:T(8,128)(2,1)S(1)}, bf16[4096,128]{1,0:T(8,128)(2,1)}, u32[]{:S(2)}) copy-start(bf16[4096,128]{1,0:T(8,128)(2,1)} %param.22) | copy-start | bytes 3145732
  266.7 21.4 %all-to-all-start.2 = ((f32[8,1,1,64,129]{4,3,2,1,0:T(8,128)}), f32[8,1,1,64,129]{4,3,2,1,0:T(8,128)S(1)}, u32[]{:S(2)}, u32[]{:S(2)}) async-start(f32[8,1,1,64,129]{4,3,2,1,0:T(8,128)} %broadcast_in_dim.28), calls=%async_computation.4 | async-start | bytes 1048576 | tf_op jit(solution)/shard_map/all_to_all | solution.py:41
  278.7 73.8 %all-gather.5.cloned.1.call-start = ((), (), s32[]{:S(2)}) async-start(), calls=%async_computation.7 | async-start | bytes 4718592 | tf_op jit(solution)/shard_map/all_gather | solution.py:63
  278.8 21.4 %copy-start.5 = (s32[4096]{0:T(1024)S(1)}, s32[4096]{0:T(1024)}, u32[]{:S(2)}) copy-start(s32[4096]{0:T(1024)} %param.23) | copy-start | bytes 49156
  278.9 21.4 %copy-start.6 = (s32[4096]{0:T(1024)S(1)}, s32[4096]{0:T(1024)}, u32[]{:S(2)}) copy-start(s32[4096]{0:T(1024)} %param.24) | copy-start | bytes 49156
  299.4 177.6 %all-gather.7.cloned.1.call-start = ((), (), s32[]{:S(2)}) async-start(), calls=%async_computation.8 | async-start | bytes 4718592 | tf_op jit(solution)/shard_map/all_gather | solution.py:63
  379.4 28.5 %copy-start.8 = (bf16[3,256,128]{2,1,0:T(8,128)(2,1)S(1)}, bf16[3,256,128]{2,1,0:T(8,128)(2,1)}, u32[]{:S(2)}) copy-start(bf16[3,256,128]{2,1,0:T(8,128)(2,1)} %param.26) | copy-start | bytes 589828
Sparse Core Ops, SparseCore 0:
  29.5 32.7 reduce-scatter.4
  194.0 39.5 reduce-scatter.2
  299.5 52.9 all-gather.4
  422.1 54.8 all-gather.6
where the time goes:
time: 496 us; the launch traced here: 495 us
  waiting for transfers between devices  139 us (28%)
  local copies, waits for them, and re-layouts  130 us (26%)
  other arithmetic  120 us (24%)
  blocking collectives  52.3 us (11%)
  starting transfers between devices  24.2 us (5%)
  between operations  14.9 us (3%)
  matrix products  14 us (3%)
    all_gather x2, waiting for transfers between devices, gather_in_order(): blocks = lax.all_gather(blocks, axes[k], axis=0, tiled=True)  91.5 us
    scatter-add x1, other arithmetic, per_device(): jax.ops.segment_sum(edge_new * live[:, None], receivers, num_segments=nod...  61 us
    reduce_scatter x1, waiting for transfers between devices, per_device(): lax.psum_scatter(pooled.astype(jnp.bfloat16), 'grp', scatter_dimension=0,...  38.6 us
    all_to_all x1, blocking collectives, summed_on_arrival(): lax.all_to_all(in_blocks(array, dim, peers), axis, 0, 0, tiled=True)  30.8 us
    gather x2, local copies, waits for them, and re-layouts, per_device(): local[receivers]  29.5 us
    gather x2, local copies, waits for them, and re-layouts, per_device(): table[fine_senders[0]]  29.5 us
    scatter-add x1, other arithmetic, per_device(): jax.ops.segment_sum(cedge_new, coarse_receivers, num_segments=owner_rows)  26.5 us
    all_gather x2, blocking collectives, gather_in_order(): blocks = lax.all_gather(blocks, axes[k], axis=0, tiled=True)  21.6 us
  transfers between devices with their start and end apart: 6, of which 4 were waited for; matrix products, arithmetic and copies ran while one was open for 38% of the time, Pallas kernels for 0%

commit v1 on v0

--- a/solution.py
+++ b/solution.py
@@ -60,7 +60,8 @@
 def gather_in_order(array, axes, order):
     blocks = array[None]
     for k in order:
-        blocks = lax.all_gather(blocks, axes[k], axis=0, tiled=True)
+        sent = jnp.stack([blocks] * lax.axis_size(axes[k]))
+        blocks = jnp.concatenate(lax.all_to_all(sent, axes[k], 0, 0), axis=0)
     current = [lax.axis_size(axes[k]) for k in reversed(order)]
     blocks = blocks.reshape(*current, *array.shape)
     turned = sorted(range(len(order)), key=lambda place: order[len(order) - 1 - place])

time: 496 us -> 593 us (1.20)
  waiting for transfers between devices: 139 us -> 221 us
  starting transfers between devices: 24.2 us -> 37 us
    all_to_all x0 -> x2, waiting for transfers between devices: none -> 173 us  [gather_in_order(): blocks = jnp.concatenate(lax.all_to_all(sent, axes[k], 0, 0), axis=0)]
    all_gather x2 -> x0, waiting for transfers between devices: 91.5 us -> none  [gather_in_order(): blocks = lax.all_gather(blocks, axes[k], axis=0, tiled=True)]
    all_gather x2 -> x0, blocking collectives: 21.6 us -> none  [gather_in_order(): blocks = lax.all_gather(blocks, axes[k], axis=0, tiled=True)]
    all_to_all x0 -> x2, blocking collectives: none -> 20.3 us  [gather_in_order(): blocks = jnp.concatenate(lax.all_to_all(sent, axes[k], 0, 0), axis=0)]
    all_to_all x0 -> x2, starting transfers between devices: none -> 13 us  [gather_in_order(): blocks = jnp.concatenate(lax.all_to_all(sent, axes[k], 0, 0), axis=0)]
    transpose x0 -> x2, local copies, waits for them, and re-layouts: none -> 9.22 us  [gather_in_order(): blocks.transpose(*turned, *range(len(order), blocks.ndim))]
    reshape x2 -> x0, local copies, waits for them, and re-layouts: 9.22 us -> none  [gather_in_order(): blocks = blocks.reshape(*current, *array.shape)]
    another operation x0 -> x4, local copies, waits for them, and re-layouts: none -> 6.06 us  [gather_in_order(): sent = jnp.stack([blocks] * lax.axis_size(axes[k]))]
  transfers between devices with their start and end apart: 6 -> 6, of which waited for: 4 -> 4; matrix products, arithmetic and copies ran while one was open for 38% -> 31% of each run, Pallas kernels for 0% -> 0%
where the time goes in v1:
time: 593 us; the launch traced here: 592 us
  waiting for transfers between devices  221 us (37%)
  local copies, waits for them, and re-layouts  133 us (22%)
  other arithmetic  120 us (20%)
  blocking collectives  51.1 us (9%)
  starting transfers between devices  37 us (6%)
  between operations  15.2 us (3%)
  matrix products  13.9 us (2%)
    all_to_all x2, waiting for transfers between devices, gather_in_order(): blocks = jnp.concatenate(lax.all_to_all(sent, axes[k], 0, 0), axis=0)  173 us
    scatter-add x1, other arithmetic, per_device(): jax.ops.segment_sum(edge_new * live[:, None], receivers, num_segments=nod...  61 us
    reduce_scatter x1, waiting for transfers between devices, per_device(): lax.psum_scatter(pooled.astype(jnp.bfloat16), 'grp', scatter_dimension=0,...  38.6 us
    all_to_all x1, blocking collectives, summed_on_arrival(): lax.all_to_all(in_blocks(array, dim, peers), axis, 0, 0, tiled=True)  30.8 us
    gather x2, local copies, waits for them, and re-layouts, per_device(): local[receivers]  29.5 us
    gather x2, local copies, waits for them, and re-layouts, per_device(): table[fine_senders[0]]  29.5 us
    scatter-add x1, other arithmetic, per_device(): jax.ops.segment_sum(cedge_new, coarse_receivers, num_segments=owner_rows)  26.5 us
    all_to_all x2, blocking collectives, gather_in_order(): blocks = jnp.concatenate(lax.all_to_all(sent, axes[k], 0, 0), axis=0)  20.3 us
  transfers between devices with their start and end apart: 6, of which 4 were waited for; matrix products, arithmetic and copies ran while one was open for 31% of the time, Pallas kernels for 0%

profile of v1, /device:TPU:1, one launch (start us, length us, event | category | flops | bytes accessed | tf_op | source)
XLA Modules:
  0.0 591.9 jit_solution(11980014177610118631)
XLA Ops:
  8.1 3.2 gather_fusion.1
  11.4 11.9 %all-to-all-start = ((bf16[32,24,128]{2,1,0:T(8,128)(2,1)}), bf16[32,24,128]{2,1,0:T(8,128)(2,1)S(1)}, u32[]{:S(2)}, u32[]{:S(2)}) async-start(bf16[32,24,128]{2,1,0:T(8,128)(2,1)} %bitcast.8), calls=%async_computation | async-start | bytes 393216 | tf_op jit(solution)/shard_map/all_to_all | solution.py:111
  24.0 4.6 scatter_custom_fusion.2
  32.2 27.0 %gather_fusion = bf16[9216,128]{1,0:T(8,128)(2,1)S(1)} fusion(bf16[768,128]{1,0:T(8,128)(2,1)S(1)} %bitcast.107, s32[9216]{0:T(1024)S(1)} %broadcast_clamp_fusion.1), kind=kCustom, calls=%fused_computation | custom fusion | bytes 4755456 | tf_op jit(solution)/shard_map/gather | solution.py:115
  61.7 4.3 copy.81
  67.1 27.0 %gather_fusion.2 = bf16[9216,128]{1,0:T(8,128)(2,1)S(1)} fusion(bf16[1536,128]{1,0:T(8,128)(2,1)S(1)} %copy.86, s32[9216]{0:T(1024)S(1)} %broadcast_clamp_fusion), kind=kCustom, calls=%fused_computation.2 | custom fusion | bytes 4755456 | tf_op jit(solution)/shard_map/gather | solution.py:115
  96.6 6.8 %fusion.114 = (f32[9216]{0:T(1024)S(1)}, f32[9216,128]{0,1:T(8,128)}) fusion(bf16[5,128,128]{2,1,0:T(8,128)(2,1)} %param.27, bf16[9216,128]{0,1:T(8,128)(2,1)} %copy.88, bf16[9216,128]{0,1:T(8,128)(2,1)} %copy.87, bf16[9216,128]{0,1:T(8,128)(2,1)} %bitcast.110, bf16[2,384,128]{2,1,0:T(8,128)(2,1)S(1)} %copy-done.8), kind=kOutput, calls=%fused_computation.141 | convolution fusion | flops 1236261888 | bytes 11964416 | tf_op jit(solution)/shard_map/dot_general | solution.py:85
  103.4 3.0 multiply_reduce_fusion
  107.2 3.0 add_multiply_fusion
  110.2 6.1 %copy.89 = f32[9216,128]{1,0:T(8,128)} copy(f32[9216,128]{0,1:T(8,128)} %add_multiply_fusion) | data formatting | bytes 9437184 | tf_op jit(solution)/shard_map/mul | solution.py:119
  116.3 61.0 %scatter_custom_fusion = f32[768,128]{1,0:T(8,128)S(1)} fusion(s32[9216]{0:T(1024)} %bitcast.122, f32[9216,128]{1,0:T(8,128)} %copy.89, f32[]{:T(128)} %constant.85.clone.1), kind=kCustom, calls=%fused_computation.68 | custom fusion | flops 1179648 | bytes 393728 | tf_op jit(solution)/shard_map/scatter-add | solution.py:118
  179.0 9.7 %scatter_custom_fusion.1 = f32[16384,128]{1,0:T(8,128)} fusion(s32[768]{0:T(1024)S(1)} %get-tuple-element.11, f32[768,128]{1,0:T(8,128)S(1)} %copy.92, f32[]{:T(128)} %constant.85.clone.1), kind=kCustom, calls=%fused_computation.19 | custom fusion | flops 98304 | bytes 8388612 | tf_op jit(solution)/shard_map/scatter-add | solution.py:132
  188.8 5.1 convert_element_type.86
  195.0 38.6 %reduce-scatter.3.cloned.1.call-done = bf16[1,32,64,128]{3,2,1,0:T(8,128)(2,1)} async-done(((bf16[8,32,64,128]{3,2,1,0:T(8,128)(2,1)}), bf16[1,32,64,128]{3,2,1,0:T(8,128)(2,1)}) %reduce-scatter.3.cloned.1.call-update) | async-done | bytes 524304 | tf_op jit(solution)/shard_map/reduce_scatter | solution.py:139
  234.9 30.8 %all_to_all.35 = bf16[32,1,1,64,129]{4,3,2,1,0:T(8,128)(2,1)S(1)} all-to-all(bf16[32,1,1,64,129]{4,3,2,1,0:T(8,128)(2,1)S(1)} %maximum_bitcast_fusion), channel_id=1, replica_groups=mesh['grp'=8,'dom_0'=4,'dom_1'=8] {'dom_0','dom_1'}, dimensions={0} | all-to-all | bytes 1056768 | tf_op jit(solution)/shard_map/all_to_all | solution.py:19
  266.7 12.0 %all-to-all-start.2 = ((f32[8,1,1,64,129]{4,3,2,1,0:T(8,128)}), f32[8,1,1,64,129]{4,3,2,1,0:T(8,128)S(1)}, u32[]{:S(2)}, u32[]{:S(2)}) async-start(f32[8,1,1,64,129]{4,3,2,1,0:T(8,128)} %broadcast_in_dim.24), calls=%async_computation.4 | async-start | bytes 1048576 | tf_op jit(solution)/shard_map/all_to_all | solution.py:41
  278.8 9.2 %all-to-all-done.2 = f32[8,1,1,64,129]{4,3,2,1,0:T(8,128)S(1)} async-done(((f32[8,1,1,64,129]{4,3,2,1,0:T(8,128)}), f32[8,1,1,64,129]{4,3,2,1,0:T(8,128)S(1)}, u32[]{:S(2)}, u32[]{:S(2)}) %all-to-all-start.2) | async-done | bytes 264224 | tf_op jit(solution)/shard_map/all_to_all | solution.py:41
  288.7 11.0 %all_to_all.36 = bf16[4,1,512,128]{3,2,1,0:T(8,128)(2,1)S(1)} all-to-all(bf16[4,1,512,128]{3,2,1,0:T(8,128)(2,1)S(1)} %stack.12), channel_id=1, replica_groups=mesh['grp'=8,'dom_0'=4,'dom_1'=8] {'dom_0'}, dimensions={0} | all-to-all | bytes 1048576 | tf_op jit(solution)/shard_map/all_to_all | solution.py:64
  299.7 3.0 stack.13
  302.6 4.9 all-to-all-start.4
  308.1 14.9 %gather_fusion.3 = bf16[4096,128]{1,0:T(8,128)(2,1)} fusion(bf16[512,128]{1,0:T(8,128)(2,1)S(1)} %copy.96, s32[4096]{0:T(1024)S(1)} %fusion.94), kind=kCustom, calls=%fused_computation.3 | custom fusion | bytes 2113536 | tf_op jit(solution)/shard_map/gather | solution.py:157
  323.0 76.5 %all-to-all-done.4 = bf16[8,4,512,128]{3,2,1,0:T(8,128)(2,1)} async-done(((bf16[8,4,512,128]{3,2,1,0:T(8,128)(2,1)}), bf16[8,4,512,128]{3,2,1,0:T(8,128)(2,1)}, u32[]{:S(2)}, u32[]{:S(2)}) %all-to-all-start.4) | async-done | bytes 4194336 | tf_op jit(solution)/shard_map/all_to_all | solution.py:64
  399.5 4.6 copy.98
  404.1 17.0 %gather_fusion.4 = bf16[4096,128]{1,0:T(8,128)(2,1)} fusion(bf16[16384,128]{1,0:T(8,128)(2,1)} %bitcast.108, s32[4096]{0:T(1024)S(1)} %fusion.95), kind=kCustom, calls=%fused_computation.4 | custom fusion | bytes 2113536 | tf_op jit(solution)/shard_map/gather | solution.py:157
  421.1 3.3 fusion.124
  428.3 26.5 %scatter_custom_fusion.3 = f32[512,128]{1,0:T(8,128)S(1)} fusion(s32[4096]{0:T(1024)S(1)} %copy-done.7, f32[4096,128]{1,0:T(8,128)S(1)} %copy.99, f32[]{:T(128)} %constant.85.clone.1), kind=kCustom, calls=%fused_computation.71 | custom fusion | flops 524288 | bytes 262148 | tf_op jit(solution)/shard_map/scatter-add | solution.py:160
  456.5 9.3 %all_to_all.37 = bf16[4,1,512,128]{3,2,1,0:T(8,128)(2,1)S(1)} all-to-all(bf16[4,1,512,128]{3,2,1,0:T(8,128)(2,1)S(1)} %stack.14), channel_id=1, replica_groups=mesh['grp'=8,'dom_0'=4,'dom_1'=8] {'dom_0'}, dimensions={0} | all-to-all | bytes 1048576 | tf_op jit(solution)/shard_map/all_to_all | solution.py:64
  465.8 3.0 stack.15
  468.8 8.1 %all-to-all-start.6 = ((bf16[8,4,512,128]{3,2,1,0:T(8,128)(2,1)}), bf16[8,4,512,128]{3,2,1,0:T(8,128)(2,1)}, u32[]{:S(2)}, u32[]{:S(2)}) async-start(bf16[8,4,512,128]{3,2,1,0:T(8,128)(2,1)} %stack.15), calls=%async_computation.8 | async-start | bytes 8388608 | tf_op jit(solution)/shard_map/all_to_all | solution.py:64
  476.9 96.8 %all-to-all-done.6 = bf16[8,4,512,128]{3,2,1,0:T(8,128)(2,1)} async-done(((bf16[8,4,512,128]{3,2,1,0:T(8,128)(2,1)}), bf16[8,4,512,128]{3,2,1,0:T(8,128)(2,1)}, u32[]{:S(2)}, u32[]{:S(2)}) %all-to-all-start.6) | async-done | bytes 4194336 | tf_op jit(solution)/shard_map/all_to_all | solution.py:64
  573.8 4.6 copy.102
  578.4 4.3 gather_fusion.5
  (90 shorter events, 25.6 us)
Async XLA Ops:
  7.2 25.0 %copy-start = (bf16[1,768,128]{2,1,0:T(8,128)(2,1)S(1)}, bf16[1,768,128]{2,1,0:T(8,128)(2,1)}, u32[]{:S(2)}) copy-start(bf16[1,768,128]{2,1,0:T(8,128)(2,1)} %param.14) | copy-start | bytes 589828
  11.4 55.3 %all-to-all-start = ((bf16[32,24,128]{2,1,0:T(8,128)(2,1)}), bf16[32,24,128]{2,1,0:T(8,128)(2,1)S(1)}, u32[]{:S(2)}, u32[]{:S(2)}) async-start(bf16[32,24,128]{2,1,0:T(8,128)(2,1)} %bitcast.8), calls=%async_computation | async-start | bytes 393216 | tf_op jit(solution)/shard_map/all_to_all | solution.py:111
  23.2 170.7 %reduce-scatter.5.cloned.1.call-start = ((), (), s32[]{:S(2)}) async-start(), calls=%async_computation.10 | async-start | bytes 73728 | tf_op jit(solution)/shard_map/reduce_scatter | solution.py:142
  29.4 204.1 %reduce-scatter.3.cloned.1.call-start = ((), (), s32[]{:S(2)}) async-start(), calls=%async_computation.9 | async-start | bytes 4718592 | tf_op jit(solution)/shard_map/reduce_scatter | solution.py:139
  94.1 2.5 copy-start.8
  96.6 9.8 %copy-start.2 = (bf16[1,9216,128]{1,2,0:T(8,128)(2,1)S(1)}, bf16[1,9216,128]{1,2,0:T(8,128)(2,1)}, u32[]{:S(2)}) copy-start(bf16[1,9216,128]{1,2,0:T(8,128)(2,1)} %copy.81) | copy-start | bytes 7077892
  103.4 3.8 copy-start.1
  194.9 83.8 %copy-start.5 = (bf16[512,128]{1,0:T(8,128)(2,1)S(1)}, bf16[512,128]{1,0:T(8,128)(2,1)}, u32[]{:S(2)}) copy-start(bf16[512,128]{1,0:T(8,128)(2,1)} %param.21) | copy-start | bytes 393220
  266.7 21.4 %all-to-all-start.2 = ((f32[8,1,1,64,129]{4,3,2,1,0:T(8,128)}), f32[8,1,1,64,129]{4,3,2,1,0:T(8,128)S(1)}, u32[]{:S(2)}, u32[]{:S(2)}) async-start(f32[8,1,1,64,129]{4,3,2,1,0:T(8,128)} %broadcast_in_dim.24), calls=%async_computation.4 | async-start | bytes 1048576 | tf_op jit(solution)/shard_map/all_to_all | solution.py:41
  302.6 4.9 copy-start.3
  302.6 5.5 copy-start.6
  302.6 5.5 copy-start.7
  302.6 96.9 %all-to-all-start.4 = ((bf16[8,4,512,128]{3,2,1,0:T(8,128)(2,1)}), bf16[8,4,512,128]{3,2,1,0:T(8,128)(2,1)}, u32[]{:S(2)}, u32[]{:S(2)}) async-start(bf16[8,4,512,128]{3,2,1,0:T(8,128)(2,1)} %stack.13), calls=%async_computation.6 | async-start | bytes 8388608 | tf_op jit(solution)/shard_map/all_to_all | solution.py:64
  426.4 28.5 %copy-start.9 = (bf16[3,256,128]{2,1,0:T(8,128)(2,1)S(1)}, bf16[3,256,128]{2,1,0:T(8,128)(2,1)}, u32[]{:S(2)}) copy-start(bf16[3,256,128]{2,1,0:T(8,128)(2,1)} %param.26) | copy-start | bytes 589828
  456.4 12.4 %copy-start.4 = (bf16[512,128]{1,0:T(8,128)(2,1)}, bf16[512,128]{1,0:T(8,128)(2,1)S(1)}, u32[]{:S(2)}) copy-start(bf16[512,128]{1,0:T(8,128)(2,1)S(1)} %copy.101) | copy-start | bytes 393220
  468.8 105.0 %all-to-all-start.6 = ((bf16[8,4,512,128]{3,2,1,0:T(8,128)(2,1)}), bf16[8,4,512,128]{3,2,1,0:T(8,128)(2,1)}, u32[]{:S(2)}, u32[]{:S(2)}) async-start(bf16[8,4,512,128]{3,2,1,0:T(8,128)(2,1)} %stack.15), calls=%async_computation.8 | async-start | bytes 8388608 | tf_op jit(solution)/shard_map/all_to_all | solution.py:64
Sparse Core Ops, SparseCore 0:
  29.5 32.7 reduce-scatter.4
  194.0 39.5 reduce-scatter.2
